TPU v7x, 32 devices: a whole 2x2x4 slice. The times are simulated.
32 devices in a mesh: dp: 4 (over x, core), fsdp: 8 (over z, y).
Axes of the slice: x: 2, y: 2, z: 4, core: 2. Of those that a mesh axis runs over, the one named last changes fastest.
Arguments:
- tokens: bfloat16 [18432, 576], P(('dp', 'fsdp')), may hold values from -6 to 6
- cotangent: bfloat16 [18432, 576], P(('dp', 'fsdp')), may hold values from -6 to 6
- w_query: bfloat16 [576, 576], P(None, 'fsdp'), may hold values from -0.25 to 0.25
- key_projection_weight: bfloat16 [576, 192], P(None, 'fsdp'), may hold values from -0.25 to 0.25
- value_projection_weight: bfloat16 [576, 192], P(None, 'fsdp'), may hold values from -0.25 to 0.25
- output_projection_weight: bfloat16 [576, 576], P(None, 'fsdp'), may hold values from -0.75 to 0.75
- w_gate: bfloat16 [576, 1536], P(None, 'fsdp'), may hold values from -0.25 to 0.25
- w_up: bfloat16 [576, 1536], P(None, 'fsdp'), may hold values from -0.25 to 0.25
- w_down: bfloat16 [1536, 576], P(None, 'fsdp'), may hold values from -0.21875 to 0.21875
- gain_attn: bfloat16 [576], P('fsdp'), may hold values from 0.099609375 to 1.8984375
- gain_mlp: bfloat16 [576], P('fsdp'), may hold values from 0.099609375 to 1.8984375
Outputs:
- output: bfloat16 [18432, 576], P(('dp', 'fsdp'))
- grad_tokens: bfloat16 [18432, 576], P(('dp', 'fsdp'))
- grad_query: float32 [576, 576], P(None, 'fsdp')
- grad_key: float32 [576, 192], P(None, 'fsdp')
- grad_value: float32 [576, 192], P(None, 'fsdp')
- grad_out: float32 [576, 576], P(None, 'fsdp')
- grad_gate: float32 [576, 1536], P(None, 'fsdp')
- grad_up: float32 [576, 1536], P(None, 'fsdp')
- grad_down: float32 [1536, 576], P(None, 'fsdp')
- grad_gain_attn: float32 [576], P('fsdp')
- grad_gain_mlp: float32 [576], P('fsdp')
All inputs are finite; a program needn't handle non-finite values.
Results may differ from a plain program's by a relative error of at most 0.017.
Values may be sent and summed in bfloat16 or wider, within the bound.
No kernel may reach another device: no remote copies, remote signals or barrier semaphores. Data moves between devices by JAX's collectives and lax.ppermute only.
A program may use at most 128 MiB of HBM per device.

v0:
```python
import jax
import jax.numpy as jnp
from jax import lax
from jax.sharding import PartitionSpec as P

QUERY_HEADS = 9
KEY_VALUE_HEADS = 3
HEAD_SIZE = 64
SEQUENCE_LENGTH = 192
EPS_NORM = 1e-05
ROPE_BASE = 100000.0


def matrix_product(left, right):
    return jnp.dot(left, right, preferred_element_type=jnp.float32)


def einsum_mixed(form, left, right):
    return jnp.einsum(form, left, right, preferred_element_type=jnp.float32)


def rope_tables(length, head):
    half = head // 2
    position = jnp.arange(length).astype(jnp.float32)
    freqs = ROPE_BASE ** (-(jnp.arange(half).astype(jnp.float32) * 2.0 / head))
    angles = position[:, None] * freqs[None, :]
    return (jnp.cos(angles)[:, None, :], jnp.sin(angles)[:, None, :])


def apply_rotary_embedding(value_rows, cosine_table, sine_table):
    half = value_rows.shape[-1] // 2
    first = value_rows[..., :half]
    second = value_rows[..., half:]
    return jnp.concatenate(
        [first * cosine_table - second * sine_table, second * cosine_table + first * sine_table], -1
    )


def reverse_rotary_embedding(value_rows, cosine_table, sine_table):
    half = value_rows.shape[-1] // 2
    first = value_rows[..., :half]
    second = value_rows[..., half:]
    return jnp.concatenate(
        [first * cosine_table + second * sine_table, second * cosine_table - first * sine_table], -1
    )


def causal_mask():
    places = jnp.arange(SEQUENCE_LENGTH)
    return places[:, None] >= places[None, :]


def layer_forward(tokens, weights, cosine_table, sine_table):
    (
        w_query,
        key_projection_weight,
        value_projection_weight,
        output_projection_weight,
        w_gate,
        w_up,
        w_down,
        gain_attn,
        gain_mlp,
    ) = weights
    token_rows = tokens.shape[0]
    sequence_count = token_rows // SEQUENCE_LENGTH
    query_group_size = QUERY_HEADS // KEY_VALUE_HEADS
    allowed = causal_mask()
    xfull = tokens.astype(jnp.float32)
    inv_one = lax.rsqrt(jnp.mean(xfull * xfull, -1, keepdims=True) + EPS_NORM)
    first_normed_input = (xfull * inv_one * gain_attn.astype(jnp.float32)).astype(jnp.bfloat16)
    query_rows = apply_rotary_embedding(
        matrix_product(first_normed_input, w_query).reshape(
            sequence_count, SEQUENCE_LENGTH, QUERY_HEADS, HEAD_SIZE
        ),
        cosine_table,
        sine_table,
    ).astype(jnp.bfloat16)
    key_rows = apply_rotary_embedding(
        matrix_product(first_normed_input, key_projection_weight).reshape(
            sequence_count, SEQUENCE_LENGTH, KEY_VALUE_HEADS, HEAD_SIZE
        ),
        cosine_table,
        sine_table,
    ).astype(jnp.bfloat16)
    value_rows = (
        matrix_product(first_normed_input, value_projection_weight)
        .reshape(sequence_count, SEQUENCE_LENGTH, KEY_VALUE_HEADS, HEAD_SIZE)
        .astype(jnp.bfloat16)
    )
    grouped_queries = query_rows.reshape(
        sequence_count, SEQUENCE_LENGTH, KEY_VALUE_HEADS, query_group_size, HEAD_SIZE
    )
    scores = einsum_mixed("nqkgd,nskd->nkgqs", grouped_queries, key_rows) * HEAD_SIZE ** (-0.5)
    expo = jnp.where(allowed, jnp.exp(jnp.where(allowed, scores, 0.0)), 0.0)
    log_total = jnp.log(jnp.sum(expo, -1, keepdims=True))
    probs = jnp.where(allowed, jnp.exp(scores - log_total), 0.0).astype(jnp.bfloat16)
    attention_output = (
        einsum_mixed("nkgqs,nskd->nqkgd", probs, value_rows)
        .reshape(token_rows, QUERY_HEADS * HEAD_SIZE)
        .astype(jnp.bfloat16)
    )
    middle = xfull + matrix_product(attention_output, output_projection_weight)
    inv_two = lax.rsqrt(jnp.mean(middle * middle, -1, keepdims=True) + EPS_NORM)
    normed_two = (middle * inv_two * gain_mlp.astype(jnp.float32)).astype(jnp.bfloat16)
    gate = matrix_product(normed_two, w_gate)
    upper = matrix_product(normed_two, w_up)
    hidden = (jax.nn.silu(gate) * upper).astype(jnp.bfloat16)
    output = (middle + matrix_product(hidden, w_down)).astype(jnp.bfloat16)
    saved = (
        xfull,
        inv_one,
        first_normed_input,
        grouped_queries,
        key_rows,
        value_rows,
        log_total,
        attention_output,
        middle,
        inv_two,
        normed_two,
        gate,
        upper,
        hidden,
    )
    return (output, saved)


def keep_local(gradients):
    return gradients


def layer_backward(cotangent, saved, weights, cosine_table, sine_table, mlp_handler):
    (
        w_query,
        key_projection_weight,
        value_projection_weight,
        output_projection_weight,
        w_gate,
        w_up,
        w_down,
        gain_attn,
        gain_mlp,
    ) = weights
    (
        xfull,
        inv_one,
        first_normed_input,
        grouped_queries,
        key_rows,
        value_rows,
        log_total,
        attention_output,
        middle,
        inv_two,
        normed_two,
        gate,
        upper,
        hidden,
    ) = saved
    token_rows = cotangent.shape[0]
    sequence_count = token_rows // SEQUENCE_LENGTH
    query_group_size = QUERY_HEADS // KEY_VALUE_HEADS
    allowed = causal_mask()
    grad_down = matrix_product(hidden.T, cotangent)
    dhidden = matrix_product(cotangent, w_down.T)
    sigma = jax.nn.sigmoid(gate)
    dgate = (dhidden * upper * sigma * (1.0 + gate * (1.0 - sigma))).astype(jnp.bfloat16)
    dupper = (dhidden * gate * sigma).astype(jnp.bfloat16)
    grad_gate = matrix_product(normed_two.T, dgate)
    grad_up = matrix_product(normed_two.T, dupper)
    dnormed_two = matrix_product(dgate, w_gate.T) + matrix_product(dupper, w_up.T)
    unit_two = middle * inv_two
    grad_gain_mlp = jnp.sum(dnormed_two * unit_two, 0)
    mlp_result = mlp_handler((grad_gate, grad_up, grad_down, grad_gain_mlp))
    scaled_two = dnormed_two * gain_mlp.astype(jnp.float32)
    dmiddle = inv_two * (
        scaled_two - unit_two * jnp.mean(scaled_two * unit_two, -1, keepdims=True)
    ) + cotangent.astype(jnp.float32)
    middle_gradient_block = dmiddle.astype(jnp.bfloat16)
    grad_out = matrix_product(attention_output.T, middle_gradient_block)
    attention_gradient = (
        matrix_product(middle_gradient_block, output_projection_weight.T)
        .astype(jnp.bfloat16)
        .reshape(sequence_count, SEQUENCE_LENGTH, KEY_VALUE_HEADS, query_group_size, HEAD_SIZE)
    )
    scores = einsum_mixed("nqkgd,nskd->nkgqs", grouped_queries, key_rows) * HEAD_SIZE ** (-0.5)
    probs = jnp.where(allowed, jnp.exp(scores - log_total), 0.0).astype(jnp.bfloat16)
    softmax_correction = jnp.sum(
        attention_gradient.astype(jnp.float32)
        * attention_output.reshape(
            sequence_count, SEQUENCE_LENGTH, KEY_VALUE_HEADS, query_group_size, HEAD_SIZE
        ).astype(jnp.float32),
        -1,
    )
    softmax_correction = jnp.transpose(softmax_correction, (0, 2, 3, 1))[..., None]
    value_gradient_rows = einsum_mixed("nkgqs,nqkgd->nskd", probs, attention_gradient)
    dprobs = einsum_mixed("nqkgd,nskd->nkgqs", attention_gradient, value_rows)
    dscores = (
        probs.astype(jnp.float32) * (dprobs - softmax_correction) * HEAD_SIZE ** (-0.5)
    ).astype(jnp.bfloat16)
    dqueries = einsum_mixed("nkgqs,nskd->nqkgd", dscores, key_rows).reshape(
        sequence_count, SEQUENCE_LENGTH, QUERY_HEADS, HEAD_SIZE
    )
    key_gradient_rows = einsum_mixed("nkgqs,nqkgd->nskd", dscores, grouped_queries)
    dq_flat = (
        reverse_rotary_embedding(dqueries, cosine_table, sine_table)
        .reshape(token_rows, QUERY_HEADS * HEAD_SIZE)
        .astype(jnp.bfloat16)
    )
    key_gradient_flat = (
        reverse_rotary_embedding(key_gradient_rows, cosine_table, sine_table)
        .reshape(token_rows, KEY_VALUE_HEADS * HEAD_SIZE)
        .astype(jnp.bfloat16)
    )
    value_gradient_flat = value_gradient_rows.reshape(
        token_rows, KEY_VALUE_HEADS * HEAD_SIZE
    ).astype(jnp.bfloat16)
    grad_query = matrix_product(first_normed_input.T, dq_flat)
    grad_key = matrix_product(first_normed_input.T, key_gradient_flat)
    grad_value = matrix_product(first_normed_input.T, value_gradient_flat)
    dnormed_one = (
        matrix_product(dq_flat, w_query.T)
        + matrix_product(key_gradient_flat, key_projection_weight.T)
        + matrix_product(value_gradient_flat, value_projection_weight.T)
    )
    unit_one = xfull * inv_one
    grad_gain_attn = jnp.sum(dnormed_one * unit_one, 0)
    scaled_one = dnormed_one * gain_attn.astype(jnp.float32)
    grad_tokens = (
        inv_one * (scaled_one - unit_one * jnp.mean(scaled_one * unit_one, -1, keepdims=True))
        + dmiddle
    ).astype(jnp.bfloat16)
    attn_result = (grad_query, grad_key, grad_value, grad_out, grad_gain_attn)
    return (grad_tokens, attn_result, mlp_result)


def body(
    tokens,
    cotangent,
    w_query,
    key_projection_weight,
    value_projection_weight,
    output_projection_weight,
    w_gate,
    w_up,
    w_down,
    gain_attn,
    gain_mlp,
):
    cosine_table, sine_table = rope_tables(SEQUENCE_LENGTH, HEAD_SIZE)
    gathered = (
        lax.all_gather(w_query, "fsdp", axis=1, tiled=True),
        lax.all_gather(key_projection_weight, "fsdp", axis=1, tiled=True),
        lax.all_gather(value_projection_weight, "fsdp", axis=1, tiled=True),
        lax.all_gather(output_projection_weight, "fsdp", axis=1, tiled=True),
        lax.all_gather(w_gate, "fsdp", axis=1, tiled=True),
        lax.all_gather(w_up, "fsdp", axis=1, tiled=True),
        lax.all_gather(w_down, "fsdp", axis=1, tiled=True),
        lax.all_gather(gain_attn, "fsdp", axis=0, tiled=True),
        lax.all_gather(gain_mlp, "fsdp", axis=0, tiled=True),
    )
    output, saved = layer_forward(tokens, gathered, cosine_table, sine_table)
    grad_tokens, attn_part, mlp_part = layer_backward(
        cotangent, saved, gathered, cosine_table, sine_table, keep_local
    )
    shares = (
        lax.psum_scatter(attn_part[0], "fsdp", scatter_dimension=1, tiled=True),
        lax.psum_scatter(attn_part[1], "fsdp", scatter_dimension=1, tiled=True),
        lax.psum_scatter(attn_part[2], "fsdp", scatter_dimension=1, tiled=True),
        lax.psum_scatter(attn_part[3], "fsdp", scatter_dimension=1, tiled=True),
        lax.psum_scatter(mlp_part[0], "fsdp", scatter_dimension=1, tiled=True),
        lax.psum_scatter(mlp_part[1], "fsdp", scatter_dimension=1, tiled=True),
        lax.psum_scatter(mlp_part[2], "fsdp", scatter_dimension=1, tiled=True),
        lax.psum_scatter(attn_part[4], "fsdp", scatter_dimension=0, tiled=True),
        lax.psum_scatter(mlp_part[3], "fsdp", scatter_dimension=0, tiled=True),
    )
    summed = (
        lax.psum(shares[0].astype(jnp.bfloat16), "dp").astype(jnp.float32),
        lax.psum(shares[1].astype(jnp.bfloat16), "dp").astype(jnp.float32),
        lax.psum(shares[2].astype(jnp.bfloat16), "dp").astype(jnp.float32),
        lax.psum(shares[3].astype(jnp.bfloat16), "dp").astype(jnp.float32),
        lax.psum(shares[4].astype(jnp.bfloat16), "dp").astype(jnp.float32),
        lax.psum(shares[5].astype(jnp.bfloat16), "dp").astype(jnp.float32),
        lax.psum(shares[6].astype(jnp.bfloat16), "dp").astype(jnp.float32),
        lax.psum(shares[7].astype(jnp.bfloat16), "dp").astype(jnp.float32),
        lax.psum(shares[8].astype(jnp.bfloat16), "dp").astype(jnp.float32),
    )
    return (
        output,
        grad_tokens,
        summed[0],
        summed[1],
        summed[2],
        summed[3],
        summed[4],
        summed[5],
        summed[6],
        summed[7],
        summed[8],
    )


def solution(mesh):
    in_specs = (
        P(("dp", "fsdp"), None),
        P(("dp", "fsdp"), None),
        P(None, "fsdp"),
        P(None, "fsdp"),
        P(None, "fsdp"),
        P(None, "fsdp"),
        P(None, "fsdp"),
        P(None, "fsdp"),
        P(None, "fsdp"),
        P("fsdp"),
        P("fsdp"),
    )
    out_specs = (
        P(("dp", "fsdp"), None),
        P(("dp", "fsdp"), None),
        P(None, "fsdp"),
        P(None, "fsdp"),
        P(None, "fsdp"),
        P(None, "fsdp"),
        P(None, "fsdp"),
        P(None, "fsdp"),
        P(None, "fsdp"),
        P("fsdp"),
        P("fsdp"),
    )
    return jax.shard_map(body, mesh=mesh, in_specs=in_specs, out_specs=out_specs, check_vma=False)
```

profile of v0, /device:TPU:0, one launch (start us, length us, event | category | flops | bytes accessed | tf_op | source)
XLA Modules:
  0.0 783.0 jit_solution(9801068825600758200)
XLA Ops:
  14.0 24.2 %all-reduce.9 = (bf16[576]{0:T(1024)(128)(2,1)S(1)}, bf16[576]{0:T(1024)(128)(2,1)}) all-reduce(bf16[576]{0:T(1024)(128)(2,1)S(1)} %dynamic-update-slice, bf16[576]{0:T(1024)(128)(2,1)S(1)} %dynamic-update-slice.1), channel_id=1, replica_groups=mesh['dp'=4,'fsdp'=8] {'fsdp'}, use_global_device_ids=true, to_apply=%add | all-reduce | flops 1152 | bytes 4608
  38.2 31.8 %all_gather.29 = bf16[576,192]{0,1:T(8,128)(2,1)S(1)} all-gather(bf16[576,24]{0,1:T(8,128)(2,1)S(1)} %copy-done.36), channel_id=1, replica_groups=mesh['dp'=4,'fsdp'=8] {'fsdp'}, dimensions={1}, use_global_device_ids=true | all-gather | bytes 248832 | tf_op jit(solution)/shard_map/all_gather | solution.py:254
  72.4 33.6 %all_gather.30 = bf16[576,576]{0,1:T(8,128)(2,1)S(1)} all-gather(bf16[576,72]{0,1:T(8,128)(2,1)S(1)} %copy-done.28), channel_id=1, replica_groups=mesh['dp'=4,'fsdp'=8] {'fsdp'}, dimensions={1}, use_global_device_ids=true | all-gather | bytes 746496 | tf_op jit(solution)/shard_map/all_gather | solution.py:253
  108.9 2.8 reshape.146
  111.8 31.4 %all_gather.28 = bf16[576,192]{0,1:T(8,128)(2,1)S(1)} all-gather(bf16[576,24]{0,1:T(8,128)(2,1)S(1)} %copy-done.37), channel_id=1, replica_groups=mesh['dp'=4,'fsdp'=8] {'fsdp'}, dimensions={1}, use_global_device_ids=true | all-gather | bytes 248832 | tf_op jit(solution)/shard_map/all_gather | solution.py:255
  147.7 2.8 fusion.3
  154.6 2.3 copy.88
  156.8 32.6 %all_gather.31 = bf16[576,576]{0,1:T(8,128)(2,1)S(1)} all-gather(bf16[576,72]{0,1:T(8,128)(2,1)S(1)} %copy-done.29), channel_id=1, replica_groups=mesh['dp'=4,'fsdp'=8] {'fsdp'}, dimensions={1}, use_global_device_ids=true | all-gather | bytes 746496 | tf_op jit(solution)/shard_map/all_gather | solution.py:256
  192.9 5.2 fusion.61
  198.0 5.2 fusion.62
  203.2 7.9 %multiply_convert_fusion = (bf16[576,1536]{1,0:T(8,128)(2,1)S(1)}, bf16[576,1536]{1,0:T(8,128)(2,1)S(1)}, bf16[576,1536]{1,0:T(8,128)(2,1)}) fusion(f32[576,1536]{1,0:T(8,128)} %fusion.61, f32[576,1536]{1,0:T(8,128)} %fusion.62, bf16[576,576]{1,0:T(8,128)(2,1)} %param.12, bf16[1536,576]{0,1:T(8,128)(2,1)} %all-gather.8.cloned.1.call-done), kind=kOutput, calls=%fused_computation.13 | convolution fusion | flops 1033371648 | bytes 14819328 | tf_op jit(solution)/shard_map/dot_general | solution.py:15
  219.9 2.8 convolution_convert_fusion.1
  222.8 3.9 reshape.170
  226.7 2.7 copy.91
  230.7 3.1 fusion.6
  237.9 3.5 convert_element_type.247
  241.5 3.2 fusion.51
  244.7 5.6 fusion.66
  250.4 5.6 fusion.67
  256.2 5.1 fusion.68
  267.4 2.2 fusion.49
  277.1 4.4 fusion.26
  281.5 17.5 %all-reduce.8 = (bf16[576]{0:T(1024)(128)(2,1)S(1)}, bf16[576]{0:T(1024)(128)(2,1)S(1)}) all-reduce(f32[576]{0:T(1024)S(1)} %get-tuple-element.46, f32[576]{0:T(1024)S(1)} %get-tuple-element.44), channel_id=9, replica_groups=mesh['dp'=4,'fsdp'=8] {'fsdp'}, use_global_device_ids=true, to_apply=%region_21.22.clone | all-reduce | flops 1152 | bytes 6912
  303.6 44.2 %reduce-scatter.22.cloned.1.call-done = f32[576,72]{0,1:T(8,128)} async-done(((f32[576,576]{0,1:T(8,128)}), f32[576,72]{0,1:T(8,128)}) %reduce-scatter.22.cloned.1.call-update) | async-done | bytes 165904
  349.4 85.5 %reduce-scatter.16.cloned.1.call-done = f32[576,192]{0,1:T(8,128)} async-done(((f32[576,1536]{0,1:T(8,128)}), f32[576,192]{0,1:T(8,128)}) %reduce-scatter.16.cloned.1.call-update) | async-done | bytes 442384 | tf_op jit(solution)/shard_map/reduce_scatter | solution.py:272
  436.7 86.2 %reduce-scatter.18.cloned.1.call-done = f32[576,192]{0,1:T(8,128)} async-done(((f32[576,1536]{0,1:T(8,128)}), f32[576,192]{0,1:T(8,128)}) %reduce-scatter.18.cloned.1.call-update) | async-done | bytes 442384 | tf_op jit(solution)/shard_map/reduce_scatter | solution.py:273
  524.6 81.0 %reduce-scatter.20.cloned.1.call-done = f32[1536,72]{0,1:T(8,128)} async-done(((f32[1536,576]{0,1:T(8,128)}), f32[1536,72]{0,1:T(8,128)}) %reduce-scatter.20.cloned.1.call-update) | async-done | bytes 442384 | tf_op jit(solution)/shard_map/reduce_scatter | solution.py:274
  607.3 3.6 add_convert_fusion
  612.1 57.2 %reduce-scatter.24.cloned.1.call-done = f32[576,24]{0,1:T(8,128)} async-done(((f32[576,192]{0,1:T(8,128)}), f32[576,24]{0,1:T(8,128)}) %reduce-scatter.24.cloned.1.call-update) | async-done | bytes 55312
  670.1 62.0 %reduce-scatter.26.cloned.1.call-done = f32[576,24]{0,1:T(8,128)} async-done(((f32[576,192]{0,1:T(8,128)}), f32[576,24]{0,1:T(8,128)}) %reduce-scatter.26.cloned.1.call-update) | async-done | bytes 55312
  732.9 10.9 %all-reduce.10 = (bf16[576,24]{0,1:T(8,128)(2,1)S(1)}, bf16[576,24]{0,1:T(8,128)(2,1)S(1)}, bf16[72]{0:T(256)(128)(2,1)S(1)}, bf16[72]{0:T(256)(128)(2,1)S(1)}) all-reduce(bf16[576,24]{0,1:T(8,128)(2,1)S(1)} %convert_element_type.255, bf16[576,24]{0,1:T(8,128)(2,1)S(1)} %convert_element_type.257, ...), channel_id=1, replica_groups=mesh['dp'=4,'fsdp'=8] {'dp'}, use_global_device_ids=true, to_apply=%region_9.10 | all-reduce | flops 27792 | bytes 111168 | tf_op jit(solution)/shard_map/psum | solution.py:280
  746.1 24.4 %all-reduce.14.cloned.1.call-done = (bf16[576,72]{0,1:T(8,128)(2,1)}, bf16[576,72]{0,1:T(8,128)(2,1)}, bf16[576,192]{0,1:T(8,128)(2,1)}, bf16[576,192]{0,1:T(8,128)(2,1)}, bf16[1536,72]{0,1:T(8,128)(2,1)}) async-done(((bf16[576,72]{0,1:T(8,128)(2,1)}, bf16[576,72]{0,1:T(8,128)(2,1)}, bf16[576,192]{0,1:T(8,128)(2,1)}, bf16[576,192]{0,1:T(8,128)(2,1)}, bf16[1536,72]{0,1:T(8,128)(2,1)}), ...) | async-done | bytes 829456 | tf_op jit(solution)/shard_map/psum | solution.py:279
  (196 shorter events, 72.9 us)
Async XLA Ops:
  7.2 5.1 copy-start.39
  7.2 6.3 copy-start.44
  7.2 6.6 copy-start.45
  7.2 31.0 %copy-start.36 = (bf16[576,24]{0,1:T(8,128)(2,1)S(1)}, bf16[576,24]{0,1:T(8,128)(2,1)}, u32[]{:S(2)}) copy-start(bf16[576,24]{0,1:T(8,128)(2,1)} %param.14) | copy-start | bytes 82948
  7.2 185.6 %all-gather.4.cloned.1.call-start = ((), (), s32[]{:S(2)}) async-start(), calls=%async_computation.7 | async-start | bytes 2211840 | tf_op jit(solution)/shard_map/all_gather | solution.py:257
  8.0 190.1 %all-gather.6.cloned.1.call-start = ((), (), s32[]{:S(2)}) async-start(), calls=%async_computation.8 | async-start | bytes 2211840 | tf_op jit(solution)/shard_map/all_gather | solution.py:258
  8.7 194.5 %all-gather.8.cloned.1.call-start = ((), (), s32[]{:S(2)}) async-start(), calls=%async_computation.9 | async-start | bytes 1990656 | tf_op jit(solution)/shard_map/all_gather | solution.py:259
  9.4 292.6 %reduce-scatter.28.cloned.1.call-start = ((), (), s32[]{:S(2)}) async-start(), calls=%async_computation.16 | async-start | bytes 1658880
  12.2 130.9 %copy-start.32 = (f32[576]{0:T(1024)}, f32[576]{0:T(1024)S(1)}, u32[]{:S(2)}) copy-start(f32[576]{0:T(1024)S(1)} %add_rsqrt_fusion.1) | copy-start | bytes 6916
  38.2 104.9 %copy-start.34 = (f32[576]{0:T(1024)}, f32[576]{0:T(1024)S(1)}, u32[]{:S(2)}) copy-start(f32[576]{0:T(1024)S(1)} %convert_element_type.224) | copy-start | bytes 6916
  111.7 32.5 %copy-start.40 = (f32[192]{0:T(256)S(1)}, f32[192]{0:T(256)}, u32[]{:S(2)}) copy-start(f32[192]{0:T(256)} %iota_convert_fusion) | copy-start | bytes 2308
  111.7 32.5 %copy-start.41 = (f32[32]{0:T(128)S(1)}, f32[32]{0:T(128)}, u32[]{:S(2)}) copy-start(f32[32]{0:T(128)} %negate_power_fusion) | copy-start | bytes 388
  146.8 3.8 copy-start.14
  152.9 4.0 copy-start.29
  191.6 21.2 %copy-start.5 = (f32[576,576]{0,1:T(8,128)}, f32[576,576]{0,1:T(8,128)S(1)}, u32[]{:S(2)}) copy-start(f32[576,576]{0,1:T(8,128)S(1)} %get-tuple-element.81) | copy-start | bytes 3981316
  203.2 7.9 %copy-start.42 = (bf16[576,1536]{0,1:T(8,128)(2,1)S(1)}, bf16[576,1536]{0,1:T(8,128)(2,1)}, u32[]{:S(2)}) copy-start(bf16[576,1536]{0,1:T(8,128)(2,1)} %all-gather.4.cloned.1.call-done) | copy-start | bytes 5308420
  219.7 128.1 %reduce-scatter.22.cloned.1.call-start = ((), (), s32[]{:S(2)}) async-start(), calls=%async_computation.13 | async-start | bytes 1658880
  230.7 3.1 copy-start.20
  237.9 3.5 copy-start.33
  237.9 3.5 copy-start.35
  244.7 190.3 %reduce-scatter.16.cloned.1.call-start = ((), (), s32[]{:S(2)}) async-start(), calls=%async_computation.10 | async-start | bytes 4423680 | tf_op jit(solution)/shard_map/reduce_scatter | solution.py:272
  250.3 272.5 %reduce-scatter.18.cloned.1.call-start = ((), (), s32[]{:S(2)}) async-start(), calls=%async_computation.11 | async-start | bytes 4423680 | tf_op jit(solution)/shard_map/reduce_scatter | solution.py:273
  256.0 349.6 %reduce-scatter.20.cloned.1.call-start = ((), (), s32[]{:S(2)}) async-start(), calls=%async_computation.12 | async-start | bytes 3981312 | tf_op jit(solution)/shard_map/reduce_scatter | solution.py:274
  261.3 407.9 %reduce-scatter.24.cloned.1.call-start = ((), (), s32[]{:S(2)}) async-start(), calls=%async_computation.14 | async-start | bytes 552960
  265.3 4.5 copy-start.1
  269.7 462.4 %reduce-scatter.26.cloned.1.call-start = ((), (), s32[]{:S(2)}) async-start(), calls=%async_computation.15 | async-start | bytes 552960
  277.0 22.1 %copy-start.3 = (f32[576,576]{0,1:T(8,128)S(1)}, f32[576,576]{0,1:T(8,128)}, u32[]{:S(2)}) copy-start(f32[576,576]{0,1:T(8,128)} %copy-done.2) | copy-start | bytes 3981316
  277.0 493.5 %all-reduce.14.cloned.1.call-start = ((), (), s32[]{:S(2)}) async-start(), calls=%async_computation.17 | async-start | bytes 1794048 | tf_op jit(solution)/shard_map/psum | solution.py:279
  349.4 257.9 %copy-start.6 = (f32[576,576]{0,1:T(8,128)S(1)}, f32[576,576]{0,1:T(8,128)}, u32[]{:S(2)}) copy-start(f32[576,576]{0,1:T(8,128)} %copy-done.5) | copy-start | bytes 3981316
  770.5 3.6 copy-start.27
  770.5 4.4 copy-start.31
  770.5 5.1 copy-start.30
  (27 other events, 47.8 us)
Sparse Core Ops, SparseCore 0:
  10.2 52.3 all-gather.3
  64.8 52.4 all-gather.5
  119.4 51.4 all-gather.7
  219.8 61.4 reduce-scatter.27
  284.7 63.0 reduce-scatter.21
  351.3 83.5 reduce-scatter.15
  438.6 84.1 reduce-scatter.17
  526.4 79.0 reduce-scatter.19
  609.4 59.7 reduce-scatter.23
  673.0 59.0 reduce-scatter.25
  735.9 34.5 all-reduce.13
where the time goes:
time: 792 us; the launch traced here: 783 us
  waiting for transfers between devices  443 us (56%)
  blocking collectives  182 us (23%)
  matrix products  75.9 us (10%)
  local copies, waits for them, and re-layouts  33.9 us (4%)
  other arithmetic  31.8 us (4%)
  between operations  16.1 us (2%)
    unnamed x15, waiting for transfers between devices  165 us
    reduce_scatter x1, waiting for transfers between devices, body(): lax.psum_scatter(mlp_part[1], 'fsdp', scatter_dimension=1, tiled=True)  86.2 us
    reduce_scatter x1, waiting for transfers between devices, body(): lax.psum_scatter(mlp_part[0], 'fsdp', scatter_dimension=1, tiled=True)  85.5 us
    reduce_scatter x1, waiting for transfers between devices, body(): lax.psum_scatter(mlp_part[2], 'fsdp', scatter_dimension=1, tiled=True)  81 us
    dot_general x21, matrix products, matrix_product(): return jnp.dot(left, right, preferred_element_type=jnp.float32)  66.5 us
    unnamed x2, blocking collectives  41.7 us
    all_gather x1, blocking collectives, body(): lax.all_gather(w_query, 'fsdp', axis=1, tiled=True)  33.6 us
    all_gather x1, blocking collectives, body(): lax.all_gather(output_projection_weight, 'fsdp', axis=1, tiled=True)  32.6 us
  transfers between devices with their start and end apart: 11, of which 7 were waited for; matrix products, arithmetic and copies ran while one was open for 15% of the time, Pallas kernels for 0%

commit v1 on v0

--- a/solution.py
+++ b/solution.py
@@ -9,6 +9,11 @@
 SEQUENCE_LENGTH = 192
 EPS_NORM = 1e-05
 ROPE_BASE = 100000.0
+
+
+def play_spot_on(w_in, mesh_dim):
+    finding = jnp.sum(lax.all_gather(w_in, mesh_dim), 0)
+    return finding
 
 
 def matrix_product(left, right):
@@ -276,7 +281,7 @@
         lax.psum_scatter(mlp_part[3], "fsdp", scatter_dimension=0, tiled=True),
     )
     summed = (
-        lax.psum(shares[0].astype(jnp.bfloat16), "dp").astype(jnp.float32),
+        play_spot_on(shares[0].astype(jnp.bfloat16), mesh_dim="dp").astype(jnp.float32),
         lax.psum(shares[1].astype(jnp.bfloat16), "dp").astype(jnp.float32),
         lax.psum(shares[2].astype(jnp.bfloat16), "dp").astype(jnp.float32),
         lax.psum(shares[3].astype(jnp.bfloat16), "dp").astype(jnp.float32),

time: 792 us -> 806 us (1.018)
  waiting for transfers between devices: 443 us -> 454 us
    unnamed x107 -> x121, local copies, waits for them, and re-layouts: 13.1 us -> 16.7 us
  transfers between devices with their start and end apart: 11 -> 11, of which waited for: 7 -> 7; matrix products, arithmetic and copies ran while one was open for 15% -> 12% of each run, Pallas kernels for 0% -> 0%
where the time goes in v1:
time: 806 us; the launch traced here: 797 us
  waiting for transfers between devices  454 us (56%)
  blocking collectives  189 us (23%)
  matrix products  72.2 us (9%)
  local copies, waits for them, and re-layouts  35.9 us (4%)
  other arithmetic  28.7 us (4%)
  between operations  16.2 us (2%)
    unnamed x15, waiting for transfers between devices  172 us
    reduce_scatter x1, waiting for transfers between devices, body(): lax.psum_scatter(mlp_part[1], 'fsdp', scatter_dimension=1, tiled=True)  86.2 us
    reduce_scatter x1, waiting for transfers between devices, body(): lax.psum_scatter(mlp_part[0], 'fsdp', scatter_dimension=1, tiled=True)  85.8 us
    reduce_scatter x1, waiting for transfers between devices, body(): lax.psum_scatter(mlp_part[2], 'fsdp', scatter_dimension=1, tiled=True)  81 us
    dot_general x21, matrix products, matrix_product(): return jnp.dot(left, right, preferred_element_type=jnp.float32)  62.2 us
    unnamed x2, blocking collectives  41.5 us
    all_gather x1, blocking collectives, body(): lax.all_gather(w_query, 'fsdp', axis=1, tiled=True)  33.5 us
    all_gather x1, blocking collectives, body(): lax.all_gather(output_projection_weight, 'fsdp', axis=1, tiled=True)  33.1 us
  transfers between devices with their start and end apart: 11, of which 7 were waited for; matrix products, arithmetic and copies ran while one was open for 12% of the time, Pallas kernels for 0%

profile of v1, /device:TPU:0, one launch (start us, length us, event | category | flops | bytes accessed | tf_op | source)
XLA Modules:
  0.0 796.9 jit_solution(6345640401729448334)
XLA Ops:
  14.0 24.2 %all-reduce.9 = (bf16[576]{0:T(1024)(128)(2,1)S(1)}, bf16[576]{0:T(1024)(128)(2,1)}) all-reduce(bf16[576]{0:T(1024)(128)(2,1)S(1)} %dynamic-update-slice, bf16[576]{0:T(1024)(128)(2,1)S(1)} %dynamic-update-slice.1), channel_id=1, replica_groups=mesh['dp'=4,'fsdp'=8] {'fsdp'}, use_global_device_ids=true, to_apply=%add | all-reduce | flops 1152 | bytes 4608
  38.2 32.0 %all_gather.35 = bf16[576,192]{0,1:T(8,128)(2,1)S(1)} all-gather(bf16[576,24]{0,1:T(8,128)(2,1)S(1)} %copy-done.42), channel_id=1, replica_groups=mesh['dp'=4,'fsdp'=8] {'fsdp'}, dimensions={1}, use_global_device_ids=true | all-gather | bytes 248832 | tf_op jit(solution)/shard_map/all_gather | solution.py:259
  72.5 33.5 %all_gather.36 = bf16[576,576]{0,1:T(8,128)(2,1)S(1)} all-gather(bf16[576,72]{0,1:T(8,128)(2,1)S(1)} %copy-done.33), channel_id=1, replica_groups=mesh['dp'=4,'fsdp'=8] {'fsdp'}, dimensions={1}, use_global_device_ids=true | all-gather | bytes 746496 | tf_op jit(solution)/shard_map/all_gather | solution.py:258
  109.0 2.8 reshape.146
  111.9 31.4 %all_gather.34 = bf16[576,192]{0,1:T(8,128)(2,1)S(1)} all-gather(bf16[576,24]{0,1:T(8,128)(2,1)S(1)} %copy-done.43), channel_id=1, replica_groups=mesh['dp'=4,'fsdp'=8] {'fsdp'}, dimensions={1}, use_global_device_ids=true | all-gather | bytes 248832 | tf_op jit(solution)/shard_map/all_gather | solution.py:260
  147.7 2.8 fusion.3
  154.5 2.3 copy.88
  156.8 33.1 %all_gather.37 = bf16[576,576]{0,1:T(8,128)(2,1)S(1)} all-gather(bf16[576,72]{0,1:T(8,128)(2,1)S(1)} %copy-done.34), channel_id=1, replica_groups=mesh['dp'=4,'fsdp'=8] {'fsdp'}, dimensions={1}, use_global_device_ids=true | all-gather | bytes 746496 | tf_op jit(solution)/shard_map/all_gather | solution.py:261
  193.4 5.2 fusion.61
  198.6 5.2 fusion.62
  203.8 7.8 multiply_convert_fusion
  214.5 2.5 multiply_reduce_fusion.1
  219.4 2.5 reshape.174
  222.0 2.7 copy.91
  226.0 3.1 fusion.6
  235.6 3.0 fusion.34
  243.9 3.6 fusion.36
  247.5 5.5 fusion.66
  253.2 5.5 fusion.67
  258.8 5.0 fusion.68
  275.1 2.4 fusion.26
  277.5 17.4 %all-reduce.8 = (bf16[576]{0:T(1024)(128)(2,1)S(1)}, bf16[576]{0:T(1024)(128)(2,1)S(1)}) all-reduce(f32[576]{0:T(1024)S(1)} %get-tuple-element.46, f32[576]{0:T(1024)S(1)} %copy-done.44), channel_id=10, replica_groups=mesh['dp'=4,'fsdp'=8] {'fsdp'}, use_global_device_ids=true, to_apply=%region_21.22.clone | all-reduce | flops 1152 | bytes 6912
  298.4 3.6 add_convert_fusion
  304.0 51.5 %reduce-scatter.26.cloned.1.call-done = f32[576,24]{0,1:T(8,128)} async-done(((f32[576,192]{0,1:T(8,128)}), f32[576,24]{0,1:T(8,128)}) %reduce-scatter.26.cloned.1.call-update) | async-done | bytes 55312
  356.3 66.3 %reduce-scatter.28.cloned.1.call-done = f32[576,72]{0,1:T(8,128)} async-done(((f32[576,576]{0,1:T(8,128)}), f32[576,72]{0,1:T(8,128)}) %reduce-scatter.28.cloned.1.call-update) | async-done | bytes 165904
  424.1 85.8 %reduce-scatter.16.cloned.1.call-done = f32[576,192]{0,1:T(8,128)} async-done(((f32[576,1536]{0,1:T(8,128)}), f32[576,192]{0,1:T(8,128)}) %reduce-scatter.16.cloned.1.call-update) | async-done | bytes 442384 | tf_op jit(solution)/shard_map/reduce_scatter | solution.py:277
  511.7 86.2 %reduce-scatter.18.cloned.1.call-done = f32[576,192]{0,1:T(8,128)} async-done(((f32[576,1536]{0,1:T(8,128)}), f32[576,192]{0,1:T(8,128)}) %reduce-scatter.18.cloned.1.call-update) | async-done | bytes 442384 | tf_op jit(solution)/shard_map/reduce_scatter | solution.py:278
  599.7 81.0 %reduce-scatter.20.cloned.1.call-done = f32[1536,72]{0,1:T(8,128)} async-done(((f32[1536,576]{0,1:T(8,128)}), f32[1536,72]{0,1:T(8,128)}) %reduce-scatter.20.cloned.1.call-update) | async-done | bytes 442384 | tf_op jit(solution)/shard_map/reduce_scatter | solution.py:279
  682.4 11.1 %all-reduce.10 = (bf16[576,24]{0,1:T(8,128)(2,1)S(1)}, bf16[576,24]{0,1:T(8,128)(2,1)S(1)}, bf16[72]{0:T(256)(128)(2,1)S(1)}, bf16[72]{0:T(256)(128)(2,1)S(1)}) all-reduce(bf16[576,24]{0,1:T(8,128)(2,1)S(1)} %convert_element_type.257, bf16[576,24]{0,1:T(8,128)(2,1)S(1)} %convert_element_type.259, ...), channel_id=1, replica_groups=mesh['dp'=4,'fsdp'=8] {'dp'}, use_global_device_ids=true, to_apply=%region_9.10 | all-reduce | flops 27792 | bytes 111168 | tf_op jit(solution)/shard_map/psum | solution.py:285
  695.8 51.6 %reduce-scatter.22.cloned.1.call-done = f32[576,72]{0,1:T(8,128)} async-done(((f32[576,576]{0,1:T(8,128)}), f32[576,72]{0,1:T(8,128)}) %reduce-scatter.22.cloned.1.call-update) | async-done | bytes 165904
  748.4 6.3 all-gather.1
  755.4 29.7 %all-reduce.14.cloned.1.call-done = (bf16[576,72]{0,1:T(8,128)(2,1)}, bf16[576,192]{0,1:T(8,128)(2,1)}, bf16[576,192]{0,1:T(8,128)(2,1)}, bf16[1536,72]{0,1:T(8,128)(2,1)}) async-done(((bf16[576,72]{0,1:T(8,128)(2,1)}, bf16[576,192]{0,1:T(8,128)(2,1)}, bf16[576,192]{0,1:T(8,128)(2,1)}, bf16[1536,72]{0,1:T(8,128)(2,1)}), (bf16[576,72]{0,1:T(8,128)(2,1)}, bf16[576,192]{0,1:T(8,128)(2,1)}, ...) | async-done | bytes 746512 | tf_op jit(solution)/shard_map/psum | solution.py:287
  (212 shorter events, 74.1 us)
Async XLA Ops:
  7.2 5.1 copy-start.46
  7.2 6.3 copy-start.51
  7.2 6.6 copy-start.52
  7.2 31.0 %copy-start.42 = (bf16[576,24]{0,1:T(8,128)(2,1)S(1)}, bf16[576,24]{0,1:T(8,128)(2,1)}, u32[]{:S(2)}) copy-start(bf16[576,24]{0,1:T(8,128)(2,1)} %param.14) | copy-start | bytes 82948
  7.2 186.2 %all-gather.6.cloned.1.call-start = ((), (), s32[]{:S(2)}) async-start(), calls=%async_computation.7 | async-start | bytes 2211840 | tf_op jit(solution)/shard_map/all_gather | solution.py:262
  8.0 190.6 %all-gather.8.cloned.1.call-start = ((), (), s32[]{:S(2)}) async-start(), calls=%async_computation.8 | async-start | bytes 2211840 | tf_op jit(solution)/shard_map/all_gather | solution.py:263
  8.7 195.1 %all-gather.10.cloned.1.call-start = ((), (), s32[]{:S(2)}) async-start(), calls=%async_computation.9 | async-start | bytes 1990656 | tf_op jit(solution)/shard_map/all_gather | solution.py:264
  9.4 293.7 %reduce-scatter.24.cloned.1.call-start = ((), (), s32[]{:S(2)}) async-start(), calls=%async_computation.14 | async-start | bytes 552960
  12.2 131.0 %copy-start.36 = (f32[576]{0:T(1024)}, f32[576]{0:T(1024)S(1)}, u32[]{:S(2)}) copy-start(f32[576]{0:T(1024)S(1)} %add_rsqrt_fusion.1) | copy-start | bytes 6916
  38.2 105.1 %copy-start.39 = (f32[576]{0:T(1024)}, f32[576]{0:T(1024)S(1)}, u32[]{:S(2)}) copy-start(f32[576]{0:T(1024)S(1)} %convert_element_type.226) | copy-start | bytes 6916
  111.8 32.5 %copy-start.47 = (f32[192]{0:T(256)S(1)}, f32[192]{0:T(256)}, u32[]{:S(2)}) copy-start(f32[192]{0:T(256)} %iota_convert_fusion) | copy-start | bytes 2308
  111.9 32.5 %copy-start.48 = (f32[32]{0:T(128)S(1)}, f32[32]{0:T(128)}, u32[]{:S(2)}) copy-start(f32[32]{0:T(128)} %negate_power_fusion) | copy-start | bytes 388
  144.6 85.5 %copy-start.27 = (f32[192,32]{0,1:T(8,128)}, f32[192,32]{0,1:T(8,128)S(1)}, u32[]{:S(2)}) copy-start(f32[192,32]{0,1:T(8,128)S(1)} %get-tuple-element.75) | copy-start | bytes 73732
  144.6 85.5 %copy-start.29 = (f32[192,32]{0,1:T(8,128)}, f32[192,32]{0,1:T(8,128)S(1)}, u32[]{:S(2)}) copy-start(f32[192,32]{0,1:T(8,128)S(1)} %get-tuple-element.76) | copy-start | bytes 73732
  146.8 3.8 copy-start.15
  152.9 4.0 copy-start.34
  192.2 24.8 %copy-start.4 = (f32[576,576]{0,1:T(8,128)}, f32[576,576]{0,1:T(8,128)S(1)}, u32[]{:S(2)}) copy-start(f32[576,576]{0,1:T(8,128)S(1)} %get-tuple-element.80) | copy-start | bytes 3981316
  203.8 7.8 copy-start.49
  226.0 3.1 copy-start.9
  226.0 3.1 copy-start.11
  230.1 3.2 copy-start.37
  230.1 3.2 copy-start.40
  235.5 119.9 %reduce-scatter.26.cloned.1.call-start = ((), (), s32[]{:S(2)}) async-start(), calls=%async_computation.15 | async-start | bytes 552960
  243.8 178.7 %reduce-scatter.28.cloned.1.call-start = ((), (), s32[]{:S(2)}) async-start(), calls=%async_computation.16 | async-start | bytes 1658880
  247.5 262.4 %reduce-scatter.16.cloned.1.call-start = ((), (), s32[]{:S(2)}) async-start(), calls=%async_computation.10 | async-start | bytes 4423680 | tf_op jit(solution)/shard_map/reduce_scatter | solution.py:277
  253.1 344.8 %reduce-scatter.18.cloned.1.call-start = ((), (), s32[]{:S(2)}) async-start(), calls=%async_computation.11 | async-start | bytes 4423680 | tf_op jit(solution)/shard_map/reduce_scatter | solution.py:278
  258.7 421.9 %reduce-scatter.20.cloned.1.call-start = ((), (), s32[]{:S(2)}) async-start(), calls=%async_computation.12 | async-start | bytes 3981312 | tf_op jit(solution)/shard_map/reduce_scatter | solution.py:279
  263.9 483.6 %reduce-scatter.22.cloned.1.call-start = ((), (), s32[]{:S(2)}) async-start(), calls=%async_computation.13 | async-start | bytes 1658880
  272.4 512.7 %all-reduce.14.cloned.1.call-start = ((), (), s32[]{:S(2)}) async-start(), calls=%async_computation.17 | async-start | bytes 1609728 | tf_op jit(solution)/shard_map/psum | solution.py:287
  275.1 19.9 %copy-start.2 = (f32[576,576]{0,1:T(8,128)S(1)}, f32[576,576]{0,1:T(8,128)}, u32[]{:S(2)}) copy-start(f32[576,576]{0,1:T(8,128)} %copy-done.1) | copy-start | bytes 3981316
  785.1 3.6 copy-start.32
  785.1 4.4 copy-start.35
  (34 other events, 49.8 us)
Sparse Core Ops, SparseCore 0:
  10.2 52.4 all-gather.5
  64.9 53.3 all-gather.7
  120.5 50.8 all-gather.9
  235.7 57.1 reduce-scatter.23
  296.6 58.8 reduce-scatter.25
  358.8 63.6 reduce-scatter.27
  426.3 83.6 reduce-scatter.15
  513.6 84.2 reduce-scatter.17
  601.6 79.0 reduce-scatter.19
  684.0 63.3 reduce-scatter.21
  751.2 33.8 all-reduce.13
